TPU v7x, 256 devices: a whole 4x4x8 slice. The times are simulated.
256 devices in a mesh: sec: 2 (over core), var: 32 (over y, z), trait: 4 (over x).
Axes of the slice: x: 4, y: 4, z: 8, core: 2. Of those that a mesh axis runs over, the one named last changes fastest.
Arguments:
- z_typed: bfloat16 [262144, 512], P(('sec', 'var'), 'trait'), may hold values from -6 to 6
- band_inverse: bfloat16 [2048, 128, 384], P(('sec', 'var')), may hold values from -0.3125 to 0.3125
- ld_untyped: bfloat16 [4096, 128, 512], P(('sec', 'var')), may hold values from -0.375 to 0.375
- trait_mix: bfloat16 [512, 512], replicated, may hold values from -0.25 to 0.25
- win_start: int32 [4096], P(('sec', 'var')), may hold values from 0 to 2047, as said below
- win_count: int32 [4096], P(('sec', 'var')), may hold values from 1 to 4, as said below
Outputs:
- imputed_mixed: bfloat16 [524288, 512], P(('sec', 'var'), 'trait')
Inputs may be any that keep to these rules, and one draw needn't show every extreme that they name: Windows follow chromosome order: within the 64 untyped blocks of one index g of sec+var, win_start never falls, and every window lies in typed blocks g * 32 - 32 to (g + 1) * 32 + 31; the first window of each index starts at its lower end (or at 0) and the last one ends at its upper end (or at the chromosome's end). win_start + win_count never exceeds 2048.
All inputs are finite; a program needn't handle non-finite values.
Results may differ from a plain program's by a relative error of at most 0.0057.
Values may be sent and summed in bfloat16 or wider, within the bound.
No kernel may reach another device: no remote copies, remote signals or barrier semaphores. Data moves between devices by JAX's collectives and lax.ppermute only.
A program may use at most 64 MiB of HBM per device.

v0:
```python
import jax
import jax.numpy as jnp
from jax import lax
from jax.sharding import PartitionSpec as P

BLK = 128
WIN = 4


def padded_2(cells, sides, width):
    for axis, dim in sides:
        count = lax.axis_size(axis)
        ends = count - 1
        head = lax.slice_in_dim(cells, 0, width, axis=dim)
        tail = lax.slice_in_dim(cells, cells.shape[dim] - width, cells.shape[dim], axis=dim)
        cells = jnp.concatenate(
            [
                lax.ppermute(tail, axis, [(i, (i + 1) % count) for i in range(ends)]),
                cells,
                lax.ppermute(head, axis, [((i + 1) % count, i) for i in range(ends)]),
            ],
            axis=dim,
        )
    return cells


def on_device(z_typed, band_inverse, ld_untyped, trait_mix, win_start, win_count):
    trait_cols = z_typed.shape[1]
    typed_blocks = z_typed.shape[0] // BLK
    padded = padded_2(z_typed, ((("sec", "var"), 0),), BLK)
    stacked = jnp.concatenate(
        [
            padded[k * BLK : (k + typed_blocks) * BLK].reshape(typed_blocks, BLK, trait_cols)
            for k in range(3)
        ],
        axis=1,
    )
    whitened = jnp.einsum(
        "bij,bjc->bic", band_inverse, stacked, preferred_element_type=jnp.float32
    ).astype(jnp.bfloat16)
    whitened_rows = whitened.reshape(typed_blocks * BLK, trait_cols)
    column_start = lax.axis_index("trait") * trait_cols
    mix_cols = lax.dynamic_slice_in_dim(trait_mix, column_start, trait_cols, 1)
    mixed_sums = jnp.dot(
        lax.all_gather(whitened_rows, "trait", axis=1, tiled=True),
        mix_cols,
        preferred_element_type=jnp.float32,
    )
    mixed = mixed_sums.astype(jnp.bfloat16).reshape(typed_blocks, BLK, trait_cols)
    window_steps = jnp.arange(WIN, dtype=jnp.int32)
    usable = window_steps[None, :] < win_count[:, None]
    untyped_blocks = win_start.shape[0]
    extended = padded_2(mixed, ((("sec", "var"), 0),), typed_blocks)
    local_first = win_start - lax.axis_index(("sec", "var")) * typed_blocks + typed_blocks
    wanted = jnp.clip(local_first[:, None] + window_steps[None, :], 0, 3 * typed_blocks - 1)
    picked = extended[wanted]
    chosen = jnp.where(usable[:, :, None, None], picked, jnp.zeros_like(picked))
    window_rows = chosen.reshape(untyped_blocks, WIN * BLK, trait_cols)
    imputed = jnp.einsum(
        "uij,ujc->uic", ld_untyped, window_rows, preferred_element_type=jnp.float32
    ).astype(jnp.bfloat16)
    return imputed.reshape(untyped_blocks * BLK, trait_cols)


def solution(mesh):
    in_specs = (
        P(("sec", "var"), "trait"),
        P(("sec", "var"), None, None),
        P(("sec", "var"), None, None),
        P(),
        P(("sec", "var")),
        P(("sec", "var")),
    )
    out_specs = P(("sec", "var"), "trait")
    return jax.shard_map(
        on_device, mesh=mesh, in_specs=in_specs, out_specs=out_specs, check_vma=False
    )
```

profile of v0, /device:TPU:24, one launch (start us, length us, event | category | flops | bytes accessed | tf_op | source)
XLA Modules:
  0.0 152.1 jit_solution(10747132638285355354)
XLA Ops:
  6.5 0.0 copy-start
  6.5 0.0 all-gather.2.cloned.1.call-start
  6.5 0.9 fusion.12
  7.5 3.9 %collective-permute-start = (bf16[128,128]{1,0:T(8,128)(2,1)S(1)}, bf16[128,128]{1,0:T(8,128)(2,1)S(1)}, u32[]{:S(2)}, u32[]{:S(2)}) collective-permute-start(bf16[128,128]{1,0:T(8,128)(2,1)S(1)} %get-tuple-element.7), channel_id=1, source_target_pairs={{0,4},{4,8},{8,12},{12,16},{16,20},{20,24},{24,28},{28,32},{32,36}... | collective-permute-start | bytes 98312 | tf_op jit(solution)/shard_map/ppermute | solution.py:18
  11.4 6.0 %collective-permute-start.1 = (bf16[128,128]{1,0:T(8,128)(2,1)S(1)}, bf16[128,128]{1,0:T(8,128)(2,1)S(1)}, u32[]{:S(2)}, u32[]{:S(2)}) collective-permute-start(bf16[128,128]{1,0:T(8,128)(2,1)S(1)} %get-tuple-element.8), channel_id=1, source_target_pairs={{4,0},{8,4},{12,8},{16,12},{20,16},{24,20},{28,24},{32,28},{36,32}... | collective-permute-start | bytes 98312 | tf_op jit(solution)/shard_map/ppermute | solution.py:20
  17.5 0.0 collective-permute-done
  17.5 1.6 %collective-permute-done.1 = bf16[128,128]{1,0:T(8,128)(2,1)S(1)} collective-permute-done((bf16[128,128]{1,0:T(8,128)(2,1)S(1)}, bf16[128,128]{1,0:T(8,128)(2,1)S(1)}, u32[]{:S(2)}, u32[]{:S(2)}) %collective-permute-start.1) | collective-permute-done | bytes 32800 | tf_op jit(solution)/shard_map/ppermute | solution.py:20
  19.0 1.7 %pad_maximum_fusion.2 = (bf16[4096,128]{1,0:T(8,128)(2,1)S(1)}, bf16[4096,128]{1,0:T(8,128)(2,1)S(1)}) fusion(bf16[4096,128]{1,0:T(8,128)(2,1)} %param.6, bf16[128,128]{1,0:T(8,128)(2,1)S(1)} %collective-permute-done, bf16[128,128]{1,0:T(8,128)(2,1)S(1)} %collective-permute-done.1), kind=kLoop, calls=%fused_computation.13 | loop fusion | flops 4194304 | bytes 3211264 | tf_op jit(solution)/shard_map/concatenate | solution.py:16
  20.7 0.0 copy-done
  20.8 3.2 %fusion.6 = bf16[32,128,128]{1,2,0:T(8,128)(2,1)} fusion(bf16[32,128,384]{2,1,0:T(8,128)(2,1)S(1)} %copy-done, bf16[32,128,128]{2,1,0:T(8,128)(2,1)S(1)} %bitcast.26, bf16[32,128,128]{2,1,0:T(8,128)(2,1)} %bitcast.24, bf16[32,128,128]{2,1,0:T(8,128)(2,1)S(1)} %bitcast.25), kind=kOutput, calls=%fused_computation.11 | convolution fusion | flops 412614656 | bytes 7340032 | tf_op jit(solution)/shard_map/bij,bjc->bic/dot_general | solution.py:38
  24.0 0.0 copy-start.1
  24.0 0.0 copy-start.2
  24.0 0.0 all-gather.2.cloned.1.call-update
  24.0 55.4 %all-gather.2.cloned.1.call-done = bf16[4096,512]{1,0:T(8,128)(2,1)} async-done(((bf16[4096,128]{1,0:T(8,128)(2,1)}), bf16[4096,512]{1,0:T(8,128)(2,1)}) %all-gather.2.cloned.1.call-update) | async-done | bytes 4194320 | tf_op jit(solution)/shard_map/all_gather | solution.py:45
  79.4 4.4 %convolution_convert_fusion = bf16[4096,128]{1,0:T(8,128)(2,1)} fusion(bf16[4096,512]{1,0:T(8,128)(2,1)} %all-gather.2.cloned.1.call-done, bf16[512,512]{1,0:T(8,128)(2,1)} %param.9, s32[]{:T(128)S(6)} %select_n.18), kind=kOutput, calls=%fused_computation.2 | convolution fusion | flops 537395200 | bytes 5373956 | tf_op jit(solution)/shard_map/dot_general | solution.py:44
  83.8 5.5 %collective-permute-start.3 = (bf16[32,128,128]{2,1,0:T(8,128)(2,1)}, bf16[32,128,128]{2,1,0:T(8,128)(2,1)}, u32[]{:S(2)}, u32[]{:S(2)}) collective-permute-start(bf16[32,128,128]{2,1,0:T(8,128)(2,1)} %bitcast.5), channel_id=1, source_target_pairs={{4,0},{8,4},{12,8},{16,12},{20,16},{24,20},{28,24},{32,28},{36,32}... | collective-permute-start | bytes 3145736 | tf_op jit(solution)/shard_map/ppermute | solution.py:20
  89.3 1.9 %collective-permute-start.2 = (bf16[32,128,128]{2,1,0:T(8,128)(2,1)}, bf16[32,128,128]{2,1,0:T(8,128)(2,1)}, u32[]{:S(2)}, u32[]{:S(2)}) collective-permute-start(bf16[32,128,128]{2,1,0:T(8,128)(2,1)} %bitcast.5), channel_id=1, source_target_pairs={{0,4},{4,8},{8,12},{12,16},{16,20},{20,24},{24,28},{28,32},{32,36}... | collective-permute-start | bytes 3145736 | tf_op jit(solution)/shard_map/ppermute | solution.py:18
  91.3 0.0 copy-done.1
  91.3 0.1 iota_compare_fusion
  91.4 0.1 broadcast_in_dim.21
  91.5 0.0 copy-done.2
  91.5 0.1 compare_select_fusion
  91.6 0.1 reshape.93
  91.8 19.4 %collective-permute-done.3 = bf16[32,128,128]{2,1,0:T(8,128)(2,1)} collective-permute-done((bf16[32,128,128]{2,1,0:T(8,128)(2,1)}, bf16[32,128,128]{2,1,0:T(8,128)(2,1)}, u32[]{:S(2)}, u32[]{:S(2)}) %collective-permute-start.3) | collective-permute-done | bytes 1048608 | tf_op jit(solution)/shard_map/ppermute | solution.py:20
  111.2 6.2 %collective-permute-done.2 = bf16[32,128,128]{2,1,0:T(8,128)(2,1)} collective-permute-done((bf16[32,128,128]{2,1,0:T(8,128)(2,1)}, bf16[32,128,128]{2,1,0:T(8,128)(2,1)}, u32[]{:S(2)}, u32[]{:S(2)}) %collective-permute-start.2) | collective-permute-done | bytes 1048608 | tf_op jit(solution)/shard_map/ppermute | solution.py:18
  117.4 3.3 %pad_maximum_fusion = bf16[96,128,128]{2,1,0:T(8,128)(2,1)} fusion(bf16[32,128,128]{2,1,0:T(8,128)(2,1)} %collective-permute-done.3, bf16[32,128,128]{2,1,0:T(8,128)(2,1)} %bitcast.5, bf16[32,128,128]{2,1,0:T(8,128)(2,1)} %collective-permute-done.2), kind=kLoop, calls=%fused_computation.9 | loop fusion | flops 3145728 | bytes 6291456 | tf_op jit(solution)/shard_map/concatenate | solution.py:16
  120.7 10.5 %gather_fusion = bf16[256,128,128]{2,1,0:T(8,128)(2,1)} fusion(bf16[96,128,128]{2,1,0:T(8,128)(2,1)} %pad_maximum_fusion, s32[1024]{0:T(1024)S(1)} %pad_clamp_fusion), kind=kCustom, calls=%fused_computation | custom fusion | bytes 16778240 | tf_op jit(solution)/shard_map/gather | solution.py:56
  131.2 7.0 %bitcast_select_fusion = bf16[64,512,128]{2,1,0:T(8,128)(2,1)S(1)} fusion(pred[64,512]{1,0:T(8,128)(4,1)S(1)} %bitcast.28, bf16[64,512,128]{2,1,0:T(8,128)(2,1)} %bitcast.23), kind=kLoop, calls=%fused_computation.1 | loop fusion | flops 4194304 | bytes 16809984 | tf_op jit(solution)/shard_map/jit(_where)/select_n | solution.py:57
  138.2 7.0 %convolution_convert_fusion.1 = bf16[64,128,128]{1,2,0:T(8,128)(2,1)} fusion(bf16[64,128,512]{2,1,0:T(8,128)(2,1)} %param.8, bf16[64,512,128]{2,1,0:T(8,128)(2,1)S(1)} %bitcast_select_fusion), kind=kOutput, calls=%fused_computation.10 | convolution fusion | flops 1074790400 | bytes 18874368 | tf_op jit(solution)/shard_map/uij,ujc->uic/dot_general | solution.py:59
  (3 shorter events, 0.0 us)
Async XLA Ops:
  6.5 14.2 %copy-start = (bf16[32,128,384]{2,1,0:T(8,128)(2,1)S(1)}, bf16[32,128,384]{2,1,0:T(8,128)(2,1)}, u32[]{:S(2)}) copy-start(bf16[32,128,384]{2,1,0:T(8,128)(2,1)} %param.7) | copy-start | bytes 9437188
  6.5 72.9 %all-gather.2.cloned.1.call-start = ((), (), s32[]{:S(2)}) async-start(), calls=%async_computation | async-start | bytes 5242880 | tf_op jit(solution)/shard_map/all_gather | solution.py:45
  7.5 10.0 %collective-permute-start = (bf16[128,128]{1,0:T(8,128)(2,1)S(1)}, bf16[128,128]{1,0:T(8,128)(2,1)S(1)}, u32[]{:S(2)}, u32[]{:S(2)}) collective-permute-start(bf16[128,128]{1,0:T(8,128)(2,1)S(1)} %get-tuple-element.7), channel_id=1, source_target_pairs={{0,4},{4,8},{8,12},{12,16},{16,20},{20,24},{24,28},{28,32},{32,36}... | collective-permute-start | bytes 98312 | tf_op jit(solution)/shard_map/ppermute | solution.py:18
  11.4 7.6 %collective-permute-start.1 = (bf16[128,128]{1,0:T(8,128)(2,1)S(1)}, bf16[128,128]{1,0:T(8,128)(2,1)S(1)}, u32[]{:S(2)}, u32[]{:S(2)}) collective-permute-start(bf16[128,128]{1,0:T(8,128)(2,1)S(1)} %get-tuple-element.8), channel_id=1, source_target_pairs={{4,0},{8,4},{12,8},{16,12},{20,16},{24,20},{28,24},{32,28},{36,32}... | collective-permute-start | bytes 98312 | tf_op jit(solution)/shard_map/ppermute | solution.py:20
  24.0 67.3 %copy-start.1 = (s32[64]{0:T(128)S(1)}, s32[64]{0:T(128)}, u32[]{:S(2)}) copy-start(s32[64]{0:T(128)} %param.11) | copy-start | bytes 772
  24.0 67.5 %copy-start.2 = (s32[64]{0:T(128)S(1)}, s32[64]{0:T(128)}, u32[]{:S(2)}) copy-start(s32[64]{0:T(128)} %param.10) | copy-start | bytes 772
  83.8 27.3 %collective-permute-start.3 = (bf16[32,128,128]{2,1,0:T(8,128)(2,1)}, bf16[32,128,128]{2,1,0:T(8,128)(2,1)}, u32[]{:S(2)}, u32[]{:S(2)}) collective-permute-start(bf16[32,128,128]{2,1,0:T(8,128)(2,1)} %bitcast.5), channel_id=1, source_target_pairs={{4,0},{8,4},{12,8},{16,12},{20,16},{24,20},{28,24},{32,28},{36,32}... | collective-permute-start | bytes 3145736 | tf_op jit(solution)/shard_map/ppermute | solution.py:20
  89.3 28.1 %collective-permute-start.2 = (bf16[32,128,128]{2,1,0:T(8,128)(2,1)}, bf16[32,128,128]{2,1,0:T(8,128)(2,1)}, u32[]{:S(2)}, u32[]{:S(2)}) collective-permute-start(bf16[32,128,128]{2,1,0:T(8,128)(2,1)} %bitcast.5), channel_id=1, source_target_pairs={{0,4},{4,8},{8,12},{12,16},{16,20},{20,24},{24,28},{28,32},{32,36}... | collective-permute-start | bytes 3145736 | tf_op jit(solution)/shard_map/ppermute | solution.py:18
Sparse Core Ops, SparseCore 0:
  24.1 55.2 all-gather.1
where the time goes:
time: 152 us
  waiting for transfers between devices  82.6 us (54%)
  starting transfers between devices  17.4 us (11%)
  matrix products  14.7 us (10%)
  between operations  13.5 us (9%)
  other arithmetic  12.2 us (8%)
  local copies, waits for them, and re-layouts  11.7 us (8%)
    all_gather x1, waiting for transfers between devices, on_device(): lax.all_gather(whitened_rows, 'trait', axis=1, tiled=True)  55.4 us
    ppermute x2, waiting for transfers between devices, padded_2(): lax.ppermute(head, axis, [((i + 1) % count, i) for i in range(ends)])  21 us
    ppermute x2, starting transfers between devices, padded_2(): lax.ppermute(head, axis, [((i + 1) % count, i) for i in range(ends)])  11.5 us
    gather x1, local copies, waits for them, and re-layouts, on_device(): picked = extended[wanted]  10.5 us
    dot_general x1, matrix products, on_device(): jnp.einsum('uij,ujc->uic', ld_untyped, window_rows, preferred_element_typ...  7.04 us
    select_n x1, other arithmetic, on_device(): chosen = jnp.where(usable[:, :, None, None], picked, jnp.zeros_like(picked))  7.01 us
    ppermute x2, waiting for transfers between devices, padded_2(): lax.ppermute(tail, axis, [(i, (i + 1) % count) for i in range(ends)])  6.23 us
    ppermute x2, starting transfers between devices, padded_2(): lax.ppermute(tail, axis, [(i, (i + 1) % count) for i in range(ends)])  5.87 us
  transfers between devices with their start and end apart: 5, of which 4 were waited for; matrix products, arithmetic and copies ran while one was open for 0% of the time, Pallas kernels for 0%

commit v1 on v0

--- a/solution.py
+++ b/solution.py
@@ -42,7 +42,10 @@
     column_start = lax.axis_index("trait") * trait_cols
     mix_cols = lax.dynamic_slice_in_dim(trait_mix, column_start, trait_cols, 1)
     mixed_sums = jnp.dot(
-        lax.all_gather(whitened_rows, "trait", axis=1, tiled=True),
+        jnp.concatenate(
+            lax.all_to_all(jnp.stack([whitened_rows] * lax.axis_size("trait")), "trait", 0, 0),
+            axis=1,
+        ),
         mix_cols,
         preferred_element_type=jnp.float32,
     )

time: 152 us -> 142 us (0.934)
  between operations: 13.5 us -> 0.16 us
  waiting for transfers between devices: 82.6 us -> 74.3 us
  local copies, waits for them, and re-layouts: 11.7 us -> 17.7 us
  starting transfers between devices: 17.4 us -> 22.8 us
    all_gather x1 -> x0, waiting for transfers between devices: 55.4 us -> none  [on_device(): lax.all_gather(whitened_rows, 'trait', axis=1, tiled=True)]
    all_to_all x0 -> x1, waiting for transfers between devices: none -> 48.3 us  [on_device(): lax.all_to_all(jnp.stack([whitened_rows] * lax.axis_size('trait')), 'trai...]
    another operation x0 -> x2, local copies, waits for them, and re-layouts: none -> 5.97 us  [on_device(): jnp.stack([whitened_rows] * lax.axis_size('trait'))]
    all_to_all x0 -> x1, starting transfers between devices: none -> 4.83 us  [on_device(): lax.all_to_all(jnp.stack([whitened_rows] * lax.axis_size('trait')), 'trai...]
where the time goes in v1:
time: 142 us
  waiting for transfers between devices  74.3 us (52%)
  starting transfers between devices  22.8 us (16%)
  local copies, waits for them, and re-layouts  17.7 us (12%)
  matrix products  14.7 us (10%)
  other arithmetic  12.1 us (9%)
    all_to_all x1, waiting for transfers between devices, on_device(): lax.all_to_all(jnp.stack([whitened_rows] * lax.axis_size('trait')), 'trai...  48.3 us
    ppermute x2, waiting for transfers between devices, padded_2(): lax.ppermute(head, axis, [((i + 1) % count, i) for i in range(ends)])  19.8 us
    ppermute x2, starting transfers between devices, padded_2(): lax.ppermute(head, axis, [((i + 1) % count, i) for i in range(ends)])  12.1 us
    gather x1, local copies, waits for them, and re-layouts, on_device(): picked = extended[wanted]  10.5 us
    dot_general x1, matrix products, on_device(): jnp.einsum('uij,ujc->uic', ld_untyped, window_rows, preferred_element_typ...  7.04 us
    select_n x1, other arithmetic, on_device(): chosen = jnp.where(usable[:, :, None, None], picked, jnp.zeros_like(picked))  7.01 us
    ppermute x2, waiting for transfers between devices, padded_2(): lax.ppermute(tail, axis, [(i, (i + 1) % count) for i in range(ends)])  6.23 us
    another operation x2, local copies, waits for them, and re-layouts, on_device(): jnp.stack([whitened_rows] * lax.axis_size('trait'))  5.97 us
  transfers between devices with their start and end apart: 5, of which 4 were waited for; matrix products, arithmetic and copies ran while one was open for 0% of the time, Pallas kernels for 0%

profile of v1, /device:TPU:24, one launch (start us, length us, event | category | flops | bytes accessed | tf_op | source)
XLA Modules:
  0.0 141.8 jit_solution(6393637339086089391)
XLA Ops:
  0.0 0.0 copy-start
  0.0 0.9 fusion.12
  0.9 3.9 %collective-permute-start = (bf16[128,128]{1,0:T(8,128)(2,1)S(1)}, bf16[128,128]{1,0:T(8,128)(2,1)S(1)}, u32[]{:S(2)}, u32[]{:S(2)}) collective-permute-start(bf16[128,128]{1,0:T(8,128)(2,1)S(1)} %get-tuple-element.7), channel_id=1, source_target_pairs={{0,4},{4,8},{8,12},{12,16},{16,20},{20,24},{24,28},{28,32},{32,36}... | collective-permute-start | bytes 98312 | tf_op jit(solution)/shard_map/ppermute | solution.py:18
  4.9 6.0 %collective-permute-start.1 = (bf16[128,128]{1,0:T(8,128)(2,1)S(1)}, bf16[128,128]{1,0:T(8,128)(2,1)S(1)}, u32[]{:S(2)}, u32[]{:S(2)}) collective-permute-start(bf16[128,128]{1,0:T(8,128)(2,1)S(1)} %get-tuple-element.8), channel_id=1, source_target_pairs={{4,0},{8,4},{12,8},{16,12},{20,16},{24,20},{28,24},{32,28},{36,32}... | collective-permute-start | bytes 98312 | tf_op jit(solution)/shard_map/ppermute | solution.py:20
  10.9 0.0 collective-permute-done
  10.9 1.6 %collective-permute-done.1 = bf16[128,128]{1,0:T(8,128)(2,1)S(1)} collective-permute-done((bf16[128,128]{1,0:T(8,128)(2,1)S(1)}, bf16[128,128]{1,0:T(8,128)(2,1)S(1)}, u32[]{:S(2)}, u32[]{:S(2)}) %collective-permute-start.1) | collective-permute-done | bytes 32800 | tf_op jit(solution)/shard_map/ppermute | solution.py:20
  12.5 1.7 %pad_maximum_fusion.2 = (bf16[4096,128]{1,0:T(8,128)(2,1)S(1)}, bf16[4096,128]{1,0:T(8,128)(2,1)S(1)}) fusion(bf16[4096,128]{1,0:T(8,128)(2,1)} %param.6, bf16[128,128]{1,0:T(8,128)(2,1)S(1)} %collective-permute-done, bf16[128,128]{1,0:T(8,128)(2,1)S(1)} %collective-permute-done.1), kind=kLoop, calls=%fused_computation.13 | loop fusion | flops 4194304 | bytes 3211264 | tf_op jit(solution)/shard_map/concatenate | solution.py:16
  14.2 0.0 copy-done
  14.2 3.2 %fusion.6 = bf16[32,128,128]{1,2,0:T(8,128)(2,1)} fusion(bf16[32,128,384]{2,1,0:T(8,128)(2,1)S(1)} %copy-done, bf16[32,128,128]{2,1,0:T(8,128)(2,1)S(1)} %bitcast.29, bf16[32,128,128]{2,1,0:T(8,128)(2,1)} %bitcast.27, bf16[32,128,128]{2,1,0:T(8,128)(2,1)S(1)} %bitcast.28), kind=kOutput, calls=%fused_computation.11 | convolution fusion | flops 412614656 | bytes 7340032 | tf_op jit(solution)/shard_map/bij,bjc->bic/dot_general | solution.py:38
  17.4 2.3 %copy.7 = bf16[4096,128]{0,1:T(8,128)(2,1)} copy(bf16[4096,128]{1,0:T(8,128)(2,1)} %bitcast.30) | data formatting | bytes 2097152 | tf_op jit(solution)/shard_map/stack;reshape | solution.py:46
  19.7 3.7 %stack.3 = bf16[4,4096,128]{1,2,0:T(8,128)(2,1)} broadcast(bf16[4096,128]{0,1:T(8,128)(2,1)} %copy.7), dimensions={1,2} | broadcast | bytes 5242880 | tf_op jit(solution)/shard_map/stack | solution.py:46
  23.4 4.8 %all-to-all-start = ((bf16[4,4096,128]{1,2,0:T(8,128)(2,1)}), bf16[4,4096,128]{1,2,0:T(8,128)(2,1)}, u32[]{:S(2)}, u32[]{:S(2)}) async-start(bf16[4,4096,128]{1,2,0:T(8,128)(2,1)} %stack.3), calls=%async_computation | async-start | bytes 8388608 | tf_op jit(solution)/shard_map/all_to_all | solution.py:46
  28.2 0.0 copy-start.1
  28.3 0.0 copy-start.2
  28.3 48.3 %all-to-all-done = bf16[4,4096,128]{1,2,0:T(8,128)(2,1)} async-done(((bf16[4,4096,128]{1,2,0:T(8,128)(2,1)}), bf16[4,4096,128]{1,2,0:T(8,128)(2,1)}, u32[]{:S(2)}, u32[]{:S(2)}) %all-to-all-start) | async-done | bytes 4194336 | tf_op jit(solution)/shard_map/all_to_all | solution.py:46
  76.5 4.5 %convolution_convert_fusion = bf16[4096,128]{1,0:T(8,128)(2,1)} fusion(bf16[4096,512]{0,1:T(8,128)(2,1)} %bitcast.6, bf16[512,512]{1,0:T(8,128)(2,1)} %param.9, s32[]{:T(128)S(6)} %select_n.18), kind=kOutput, calls=%fused_computation.2 | convolution fusion | flops 537395200 | bytes 5373956 | tf_op jit(solution)/shard_map/dot_general | solution.py:44
  81.0 6.0 %collective-permute-start.3 = (bf16[32,128,128]{2,1,0:T(8,128)(2,1)}, bf16[32,128,128]{2,1,0:T(8,128)(2,1)}, u32[]{:S(2)}, u32[]{:S(2)}) collective-permute-start(bf16[32,128,128]{2,1,0:T(8,128)(2,1)} %bitcast.7), channel_id=1, source_target_pairs={{4,0},{8,4},{12,8},{16,12},{20,16},{24,20},{28,24},{32,28},{36,32}... | collective-permute-start | bytes 3145736 | tf_op jit(solution)/shard_map/ppermute | solution.py:20
  87.0 1.9 %collective-permute-start.2 = (bf16[32,128,128]{2,1,0:T(8,128)(2,1)}, bf16[32,128,128]{2,1,0:T(8,128)(2,1)}, u32[]{:S(2)}, u32[]{:S(2)}) collective-permute-start(bf16[32,128,128]{2,1,0:T(8,128)(2,1)} %bitcast.7), channel_id=1, source_target_pairs={{0,4},{4,8},{8,12},{12,16},{16,20},{20,24},{24,28},{28,32},{32,36}... | collective-permute-start | bytes 3145736 | tf_op jit(solution)/shard_map/ppermute | solution.py:18
  89.0 0.0 copy-done.1
  89.0 0.1 iota_compare_fusion
  89.1 0.1 broadcast_in_dim.21
  89.2 0.0 copy-done.2
  89.3 0.1 compare_select_fusion
  89.3 0.1 reshape.99
  89.5 18.2 %collective-permute-done.3 = bf16[32,128,128]{2,1,0:T(8,128)(2,1)} collective-permute-done((bf16[32,128,128]{2,1,0:T(8,128)(2,1)}, bf16[32,128,128]{2,1,0:T(8,128)(2,1)}, u32[]{:S(2)}, u32[]{:S(2)}) %collective-permute-start.3) | collective-permute-done | bytes 1048608 | tf_op jit(solution)/shard_map/ppermute | solution.py:20
  107.7 6.2 %collective-permute-done.2 = bf16[32,128,128]{2,1,0:T(8,128)(2,1)} collective-permute-done((bf16[32,128,128]{2,1,0:T(8,128)(2,1)}, bf16[32,128,128]{2,1,0:T(8,128)(2,1)}, u32[]{:S(2)}, u32[]{:S(2)}) %collective-permute-start.2) | collective-permute-done | bytes 1048608 | tf_op jit(solution)/shard_map/ppermute | solution.py:18
  113.9 3.3 %pad_maximum_fusion = bf16[96,128,128]{2,1,0:T(8,128)(2,1)} fusion(bf16[32,128,128]{2,1,0:T(8,128)(2,1)} %collective-permute-done.3, bf16[32,128,128]{2,1,0:T(8,128)(2,1)} %bitcast.7, bf16[32,128,128]{2,1,0:T(8,128)(2,1)} %collective-permute-done.2), kind=kLoop, calls=%fused_computation.9 | loop fusion | flops 3145728 | bytes 6291456 | tf_op jit(solution)/shard_map/concatenate | solution.py:16
  117.2 10.5 %gather_fusion = bf16[256,128,128]{2,1,0:T(8,128)(2,1)} fusion(bf16[96,128,128]{2,1,0:T(8,128)(2,1)} %pad_maximum_fusion, s32[1024]{0:T(1024)S(1)} %pad_clamp_fusion), kind=kCustom, calls=%fused_computation | custom fusion | bytes 16778240 | tf_op jit(solution)/shard_map/gather | solution.py:59
  127.7 7.0 %bitcast_select_fusion = bf16[64,512,128]{2,1,0:T(8,128)(2,1)S(1)} fusion(pred[64,512]{1,0:T(8,128)(4,1)S(1)} %bitcast.31, bf16[64,512,128]{2,1,0:T(8,128)(2,1)} %bitcast.26), kind=kLoop, calls=%fused_computation.1 | loop fusion | flops 4194304 | bytes 16809984 | tf_op jit(solution)/shard_map/jit(_where)/select_n | solution.py:60
  134.7 7.0 %convolution_convert_fusion.1 = bf16[64,128,128]{1,2,0:T(8,128)(2,1)} fusion(bf16[64,128,512]{2,1,0:T(8,128)(2,1)} %param.8, bf16[64,512,128]{2,1,0:T(8,128)(2,1)S(1)} %bitcast_select_fusion), kind=kOutput, calls=%fused_computation.10 | convolution fusion | flops 1074790400 | bytes 18874368 | tf_op jit(solution)/shard_map/uij,ujc->uic/dot_general | solution.py:62
  (3 shorter events, 0.0 us)
Async XLA Ops:
  0.0 14.2 %copy-start = (bf16[32,128,384]{2,1,0:T(8,128)(2,1)S(1)}, bf16[32,128,384]{2,1,0:T(8,128)(2,1)}, u32[]{:S(2)}) copy-start(bf16[32,128,384]{2,1,0:T(8,128)(2,1)} %param.7) | copy-start | bytes 9437188
  0.9 10.0 %collective-permute-start = (bf16[128,128]{1,0:T(8,128)(2,1)S(1)}, bf16[128,128]{1,0:T(8,128)(2,1)S(1)}, u32[]{:S(2)}, u32[]{:S(2)}) collective-permute-start(bf16[128,128]{1,0:T(8,128)(2,1)S(1)} %get-tuple-element.7), channel_id=1, source_target_pairs={{0,4},{4,8},{8,12},{12,16},{16,20},{20,24},{24,28},{28,32},{32,36}... | collective-permute-start | bytes 98312 | tf_op jit(solution)/shard_map/ppermute | solution.py:18
  4.9 7.6 %collective-permute-start.1 = (bf16[128,128]{1,0:T(8,128)(2,1)S(1)}, bf16[128,128]{1,0:T(8,128)(2,1)S(1)}, u32[]{:S(2)}, u32[]{:S(2)}) collective-permute-start(bf16[128,128]{1,0:T(8,128)(2,1)S(1)} %get-tuple-element.8), channel_id=1, source_target_pairs={{4,0},{8,4},{12,8},{16,12},{20,16},{24,20},{28,24},{32,28},{36,32}... | collective-permute-start | bytes 98312 | tf_op jit(solution)/shard_map/ppermute | solution.py:20
  23.4 53.1 %all-to-all-start = ((bf16[4,4096,128]{1,2,0:T(8,128)(2,1)}), bf16[4,4096,128]{1,2,0:T(8,128)(2,1)}, u32[]{:S(2)}, u32[]{:S(2)}) async-start(bf16[4,4096,128]{1,2,0:T(8,128)(2,1)} %stack.3), calls=%async_computation | async-start | bytes 8388608 | tf_op jit(solution)/shard_map/all_to_all | solution.py:46
  28.2 60.7 %copy-start.1 = (s32[64]{0:T(128)S(1)}, s32[64]{0:T(128)}, u32[]{:S(2)}) copy-start(s32[64]{0:T(128)} %param.11) | copy-start | bytes 772
  28.3 61.0 %copy-start.2 = (s32[64]{0:T(128)S(1)}, s32[64]{0:T(128)}, u32[]{:S(2)}) copy-start(s32[64]{0:T(128)} %param.10) | copy-start | bytes 772
  81.0 26.7 %collective-permute-start.3 = (bf16[32,128,128]{2,1,0:T(8,128)(2,1)}, bf16[32,128,128]{2,1,0:T(8,128)(2,1)}, u32[]{:S(2)}, u32[]{:S(2)}) collective-permute-start(bf16[32,128,128]{2,1,0:T(8,128)(2,1)} %bitcast.7), channel_id=1, source_target_pairs={{4,0},{8,4},{12,8},{16,12},{20,16},{24,20},{28,24},{32,28},{36,32}... | collective-permute-start | bytes 3145736 | tf_op jit(solution)/shard_map/ppermute | solution.py:20
  87.0 26.9 %collective-permute-start.2 = (bf16[32,128,128]{2,1,0:T(8,128)(2,1)}, bf16[32,128,128]{2,1,0:T(8,128)(2,1)}, u32[]{:S(2)}, u32[]{:S(2)}) collective-permute-start(bf16[32,128,128]{2,1,0:T(8,128)(2,1)} %bitcast.7), channel_id=1, source_target_pairs={{0,4},{4,8},{8,12},{12,16},{16,20},{20,24},{24,28},{28,32},{32,36}... | collective-permute-start | bytes 3145736 | tf_op jit(solution)/shard_map/ppermute | solution.py:18
